TPU v7x, 512 devices: a whole 4x8x8 slice. The times are simulated.
512 devices in a mesh: frame: 16 (over y, core), tok: 32 (over x, z).
Axes of the slice: x: 4, y: 8, z: 8, core: 2. Of those that a mesh axis runs over, the one named last changes fastest.
Arguments:
- inputs: bfloat16 [16, 24576, 512], P('frame', 'tok'), may hold values from -16 to 16
- kv_weight: bfloat16 [512, 2048], replicated, may hold values from -0.25 to 0.25
- latent_queries: bfloat16 [1024, 1024], P('tok'), may hold values from -21 to 21
- mix_gain: float32 [3072], replicated, may hold values from 0.5 to 2
- mix_weight: bfloat16 [3072, 1024], P(None, 'tok'), may hold values from -0.109375 to 0.109375
- output_queries: bfloat16 [16, 4096, 1024], P('frame', 'tok'), may hold values from -28 to 28
Outputs:
- decoded: float32 [16, 4096, 1024], P('frame', 'tok')
All inputs are finite; a program needn't handle non-finite values.
Results may differ from a plain program's by a relative error of at most 0.035.
Values may be sent and summed in bfloat16 or wider, within the bound.
No kernel may reach another device: no remote copies, remote signals or barrier semaphores. Data moves between devices by JAX's collectives and lax.ppermute only.
A program may use at most 128 MiB of HBM per device.

v0:
```python
import math
import jax
import jax.numpy as jnp
from jax import lax
from jax.sharding import PartitionSpec as P

HEADS = 8
HEAD_DIM = 128


def from_behind(block, axis, distance):
    devices = range(lax.axis_size(axis))
    route = [(i - distance, i) for i in devices if i - distance in devices]
    return lax.ppermute(block, axis, route)


def attend_heads(queries, keys, values, head_count, head_dim):
    maxima = []
    numers = []
    denoms = []
    for head_index in range(head_count):
        low_col = head_index * head_dim
        high_col = low_col + head_dim
        scores = lax.dot_general(
            queries[:, low_col:high_col],
            keys[:, low_col:high_col],
            (((1,), (1,)), ((), ())),
            preferred_element_type=jnp.float32,
        ) / math.sqrt(head_dim)
        row_peak = jnp.max(scores, axis=1)
        weights = jnp.exp(scores - row_peak[:, None])
        denoms.append(jnp.sum(weights, axis=1))
        numers.append(
            jnp.dot(
                weights.astype(jnp.bfloat16),
                values[:, low_col:high_col],
                preferred_element_type=jnp.float32,
            )
        )
        maxima.append(row_peak)
    return (jnp.stack(maxima, axis=1), jnp.concatenate(numers, axis=1), jnp.stack(denoms, axis=1))


def finish_latents(numerator, denominator, head_count, head_dim):
    row_count = numerator.shape[0]
    shaped = numerator.reshape(row_count, head_count, head_dim) / denominator[:, :, None]
    return shaped.reshape(row_count, head_count * head_dim).astype(jnp.bfloat16)


def project_cols(latent_part, gain_part, weight_part):
    scaled = (latent_part.astype(jnp.float32) * gain_part).astype(jnp.bfloat16)
    return lax.dot_general(
        weight_part, scaled, (((0,), (1,)), ((), ())), preferred_element_type=jnp.float32
    )


def local(inputs, kv_weight, latent_queries, mix_gain, mix_weight, output_queries):
    head_count = HEADS
    head_dim = HEAD_DIM
    latent_width = head_count * head_dim
    frame_inputs = inputs[0]
    queries = lax.all_gather(latent_queries, "tok", axis=0, tiled=True)
    key_values = jnp.dot(frame_inputs, kv_weight, preferred_element_type=jnp.float32).astype(
        jnp.bfloat16
    )
    maxima, numers, denoms = attend_heads(
        queries, key_values[:, :latent_width], key_values[:, latent_width:], head_count, head_dim
    )
    peak_all = lax.pmax(maxima.astype(jnp.bfloat16), "tok").astype(maxima.dtype)
    rescale = jnp.exp(maxima - peak_all)
    latent_count = queries.shape[0]
    numer_terms = (
        numers.reshape(latent_count, head_count, head_dim) * rescale[:, :, None]
    ).reshape(latent_count, latent_width)
    denom_terms = denoms * rescale
    numerator, denominator = (
        lax.psum(numer_terms.astype(jnp.bfloat16), "tok").astype(jnp.float32),
        lax.psum(denom_terms.astype(jnp.bfloat16), "tok").astype(jnp.float32),
    )
    latents = finish_latents(numerator, denominator, head_count, head_dim)
    prior_one = from_behind(latents, "frame", 1)
    prior_two = from_behind(latents, "frame", 2)
    joined = jnp.concatenate([latents, prior_one, prior_two], axis=1)
    joined_f32 = joined.astype(jnp.float32)
    squares = jnp.sum(joined_f32 * joined_f32, axis=1)
    summed = project_cols(joined, mix_gain, mix_weight)
    inverse = lax.rsqrt(squares / (3 * latent_width) + 1e-06)
    mixed_cols = jax.nn.gelu(summed * inverse[None, :], approximate=False).astype(jnp.bfloat16)
    mixed_t = lax.all_gather(mixed_cols, "tok", axis=0, tiled=True)
    frame_queries = output_queries[0]
    pieces = []
    for head_index in range(head_count):
        low_col = head_index * head_dim
        high_col = low_col + head_dim
        scores = jnp.dot(
            frame_queries[:, low_col:high_col],
            mixed_t[low_col:high_col],
            preferred_element_type=jnp.float32,
        ) / math.sqrt(head_dim)
        row_peak = jnp.max(scores, axis=1)
        weights = jnp.exp(scores - row_peak[:, None])
        denom_sum = jnp.sum(weights, axis=1)
        head_sum = lax.dot_general(
            weights.astype(jnp.bfloat16),
            mixed_t[low_col:high_col],
            (((1,), (1,)), ((), ())),
            preferred_element_type=jnp.float32,
        )
        pieces.append(head_sum / denom_sum[:, None])
    result = jnp.concatenate(pieces, axis=1)
    return result[None]


def solution(mesh):
    return jax.shard_map(
        local,
        mesh=mesh,
        in_specs=(
            P("frame", "tok", None),
            P(),
            P("tok", None),
            P(),
            P(None, "tok"),
            P("frame", "tok", None),
        ),
        out_specs=P("frame", "tok", None),
        check_vma=False,
    )
```

profile of v0, /device:TPU:8, one launch (start us, length us, event | category | flops | bytes accessed | tf_op | source)
XLA Modules:
  0.0 638.2 jit_solution(1912989845370051976)
XLA Ops:
  8.1 4.6 convolution_convert_fusion
  12.7 86.4 %all-gather.3.cloned.1.call-done = bf16[1024,1024]{1,0:T(8,128)(2,1)} async-done(((bf16[32,1024]{1,0:T(8,128)(2,1)}), bf16[1024,1024]{1,0:T(8,128)(2,1)}) %all-gather.3.cloned.1.call-update) | async-done | bytes 2097168 | tf_op jit(solution)/shard_map/all_gather | solution.py:62
  101.3 2.4 fusion.55
  105.9 2.1 multiply_reduce_fusion.5
  114.0 2.1 multiply_reduce_fusion.2
  116.6 2.1 multiply_reduce_fusion.1
  123.8 140.2 %pmax.7 = bf16[1024,8]{0,1:T(8,128)(2,1)S(1)} all-reduce(bf16[1024,8]{0,1:T(8,128)(2,1)S(1)} %convert_element_type.107), channel_id=1, replica_groups=mesh['frame'=16,'tok'=32] {'tok'}, use_global_device_ids=true, to_apply=%region_8.0 | all-reduce | flops 8192 | bytes 32768 | tf_op jit(solution)/shard_map/pmax | solution.py:69
  264.0 3.6 fusion.58
  267.6 2.6 fusion.61
  270.2 2.6 fusion.64
  272.8 2.6 fusion.67
  275.4 2.6 fusion.70
  278.0 2.4 fusion.73
  280.4 2.4 fusion.76
  282.9 4.1 fusion.6
  287.1 138.0 %psum.15 = bf16[1024,8]{0,1:T(8,128)(2,1)S(1)} all-reduce(bf16[1024,8]{0,1:T(8,128)(2,1)S(1)} %get-tuple-element.5), channel_id=1, replica_groups=mesh['frame'=16,'tok'=32] {'tok'}, use_global_device_ids=true, to_apply=%region_18.0 | all-reduce | flops 8192 | bytes 32768 | tf_op jit(solution)/shard_map/psum | solution.py:78
  425.1 21.8 %all-reduce.2.cloned.1.call-done = bf16[1024,1024]{0,1:T(8,128)(2,1)} async-done(((bf16[1024,1024]{0,1:T(8,128)(2,1)}), bf16[1024,1024]{0,1:T(8,128)(2,1)}) %all-reduce.2.cloned.1.call-update) | async-done | bytes 2097168 | tf_op jit(solution)/shard_map/psum | solution.py:77
  446.9 2.2 fusion.5
  451.2 3.6 collective-permute-start.1
  454.8 41.8 %collective-permute-done = bf16[1024,1024]{0,1:T(8,128)(2,1)S(1)} collective-permute-done((bf16[1024,1024]{0,1:T(8,128)(2,1)S(1)}, bf16[1024,1024]{0,1:T(8,128)(2,1)S(1)}, u32[]{:S(2)}, u32[]{:S(2)}) %collective-permute-start) | collective-permute-done | bytes 2097184 | tf_op jit(solution)/shard_map/ppermute | solution.py:14
  496.6 5.0 collective-permute-done.1
  501.6 11.4 %fusion.1 = f32[1024]{0:T(1024)S(1)} fusion(bf16[1024,1024]{0,1:T(8,128)(2,1)S(1)} %collective-permute-done.1, bf16[1024,1024]{0,1:T(8,128)(2,1)S(1)} %collective-permute-done, bf16[1024,1024]{0,1:T(8,128)(2,1)S(1)} %fusion.5), kind=kLoop, calls=%fused_computation.3 | loop fusion | flops 25164800 | bytes 6295552 | tf_op jit(solution)/shard_map/reduce_sum | solution.py:85
  513.0 2.4 fusion.173
  515.4 101.5 %all-gather.5.cloned.1.call-done = bf16[1024,1024]{1,0:T(8,128)(2,1)} async-done(((bf16[32,1024]{1,0:T(8,128)(2,1)}), bf16[1024,1024]{1,0:T(8,128)(2,1)}) %all-gather.5.cloned.1.call-update) | async-done | bytes 2097168 | tf_op jit(solution)/shard_map/all_gather | solution.py:89
  (85 shorter events, 34.3 us)
Async XLA Ops:
  6.5 1.6 copy-start
  6.5 92.6 %all-gather.3.cloned.1.call-start = ((), (), s32[]{:S(2)}) async-start(), calls=%async_computation | async-start | bytes 2162688 | tf_op jit(solution)/shard_map/all_gather | solution.py:62
  7.3 439.6 %all-reduce.2.cloned.1.call-start = ((), (), s32[]{:S(2)}) async-start(), calls=%async_computation.1 | async-start | bytes 4194304 | tf_op jit(solution)/shard_map/psum | solution.py:77
  105.4 2.7 copy-start.1
  108.1 2.7 copy-start.2
  110.7 2.7 copy-start.4
  113.4 2.7 copy-start.6
  116.1 2.7 copy-start.8
  118.8 2.7 copy-start.10
  121.4 1.7 copy-start.12
  264.0 3.6 copy-start.3
  264.0 6.2 copy-start.5
  267.6 5.2 copy-start.7
  270.2 5.2 copy-start.9
  272.8 5.2 copy-start.11
  275.4 5.0 copy-start.13
  287.1 329.9 %all-gather.5.cloned.1.call-start = ((), (), s32[]{:S(2)}) async-start(), calls=%async_computation.2 | async-start | bytes 2162688 | tf_op jit(solution)/shard_map/all_gather | solution.py:89
  449.1 63.9 %copy-start.15 = (bf16[3072,32]{0,1:T(8,128)(2,1)S(1)}, bf16[3072,32]{0,1:T(8,128)(2,1)}, u32[]{:S(2)}) copy-start(bf16[3072,32]{0,1:T(8,128)(2,1)} %param.10) | copy-start | bytes 589828
  449.1 63.9 %copy-start.16 = (f32[3072]{0:T(1024)S(1)}, f32[3072]{0:T(1024)}, u32[]{:S(2)}) copy-start(f32[3072]{0:T(1024)} %param.9) | copy-start | bytes 36868
  449.1 47.4 %collective-permute-start = (bf16[1024,1024]{0,1:T(8,128)(2,1)S(1)}, bf16[1024,1024]{0,1:T(8,128)(2,1)S(1)}, u32[]{:S(2)}, u32[]{:S(2)}) collective-permute-start(bf16[1024,1024]{0,1:T(8,128)(2,1)S(1)} %fusion.5), channel_id=1, source_target_pairs={{0,32},{32,64},{64,96},{96,128},{128,160},{160,192},{192,224},{224... | collective-permute-start | bytes 6291464 | tf_op jit(solution)/shard_map/ppermute | solution.py:14
  451.2 50.4 %collective-permute-start.1 = (bf16[1024,1024]{0,1:T(8,128)(2,1)S(1)}, bf16[1024,1024]{0,1:T(8,128)(2,1)S(1)}, u32[]{:S(2)}, u32[]{:S(2)}) collective-permute-start(bf16[1024,1024]{0,1:T(8,128)(2,1)S(1)} %fusion.5), channel_id=1, source_target_pairs={{0,64},{32,96},{64,128},{96,160},{128,192},{160,224},{192,256},{22... | collective-permute-start | bytes 6291464 | tf_op jit(solution)/shard_map/ppermute | solution.py:14
  622.5 6.1 copy-start.14
Sparse Core Ops, SparseCore 0:
  10.5 88.5 all-gather.2
  287.2 159.6 all-reduce.1
  515.5 101.3 all-gather.4
where the time goes:
time: 639 us; the launch traced here: 638 us
  blocking collectives  278 us (44%)
  waiting for transfers between devices  257 us (40%)
  matrix products  56.4 us (9%)
  other arithmetic  23.4 us (4%)
  between operations  13.4 us (2%)
    pmax x1, blocking collectives, local(): peak_all = lax.pmax(maxima.astype(jnp.bfloat16), 'tok').astype(maxima.dtype)  140 us
    psum x1, blocking collectives, local(): lax.psum(denom_terms.astype(jnp.bfloat16), 'tok').astype(jnp.float32)  138 us
    all_gather x1, waiting for transfers between devices, local(): mixed_t = lax.all_gather(mixed_cols, 'tok', axis=0, tiled=True)  102 us
    all_gather x1, waiting for transfers between devices, local(): queries = lax.all_gather(latent_queries, 'tok', axis=0, tiled=True)  86.4 us
    ppermute x2, waiting for transfers between devices, from_behind(): return lax.ppermute(block, axis, route)  46.8 us
    psum x1, waiting for transfers between devices, local(): lax.psum(numer_terms.astype(jnp.bfloat16), 'tok').astype(jnp.float32)  21.8 us
    dot_general x8, matrix products, attend_heads(): jnp.dot(weights.astype(jnp.bfloat16), values[:, low_col:high_col], prefer...  21.2 us
    dot_general x8, matrix products, attend_heads(): lax.dot_general(queries[:, low_col:high_col], keys[:, low_col:high_col],...  15.8 us
  transfers between devices with their start and end apart: 5, of which 5 were waited for; matrix products, arithmetic and copies ran while one was open for 1% of the time, Pallas kernels for 0%

commit v1 on v0

--- a/solution.py
+++ b/solution.py
@@ -86,7 +86,9 @@
     summed = project_cols(joined, mix_gain, mix_weight)
     inverse = lax.rsqrt(squares / (3 * latent_width) + 1e-06)
     mixed_cols = jax.nn.gelu(summed * inverse[None, :], approximate=False).astype(jnp.bfloat16)
-    mixed_t = lax.all_gather(mixed_cols, "tok", axis=0, tiled=True)
+    mixed_t = jnp.concatenate(
+        lax.all_to_all(jnp.stack([mixed_cols] * lax.axis_size("tok")), "tok", 0, 0), axis=0
+    )
     frame_queries = output_queries[0]
     pieces = []
     for head_index in range(head_count):

time: 639 us -> 589 us (0.922)
  the two profiles are of different devices: /device:TPU:8 before, /device:TPU:97 now
where the time goes in v1:
time: 589 us; the launch traced here: 588 us
  blocking collectives  261 us (44%)
  waiting for transfers between devices  227 us (39%)
  matrix products  48 us (8%)
  other arithmetic  23.4 us (4%)
  between operations  13.8 us (2%)
  starting transfers between devices  9.94 us (2%)
    psum x1, blocking collectives, local(): lax.psum(denom_terms.astype(jnp.bfloat16), 'tok').astype(jnp.float32)  113 us
    pmax x1, blocking collectives, local(): peak_all = lax.pmax(maxima.astype(jnp.bfloat16), 'tok').astype(maxima.dtype)  109 us
    all_gather x1, waiting for transfers between devices, local(): queries = lax.all_gather(latent_queries, 'tok', axis=0, tiled=True)  79.8 us
    psum x1, waiting for transfers between devices, local(): lax.psum(numer_terms.astype(jnp.bfloat16), 'tok').astype(jnp.float32)  78 us
    ppermute x2, waiting for transfers between devices, from_behind(): return lax.ppermute(block, axis, route)  68.3 us
    all_to_all x1, blocking collectives, local(): lax.all_to_all(jnp.stack([mixed_cols] * lax.axis_size('tok')), 'tok', 0, 0)  38.8 us
    dot_general x8, matrix products, attend_heads(): jnp.dot(weights.astype(jnp.bfloat16), values[:, low_col:high_col], prefer...  21.2 us
    dot_general x8, matrix products, attend_heads(): lax.dot_general(queries[:, low_col:high_col], keys[:, low_col:high_col],...  15.8 us
  transfers between devices with their start and end apart: 4, of which 4 were waited for; matrix products, arithmetic and copies ran while one was open for 1% of the time, Pallas kernels for 0%

profile of v1, /device:TPU:97, one launch (start us, length us, event | category | flops | bytes accessed | tf_op | source)
XLA Modules:
  0.0 587.8 jit_solution(7069232143020674691)
XLA Ops:
  8.1 4.6 convolution_convert_fusion
  12.7 79.8 %all-gather.2.cloned.1.call-done = bf16[1024,1024]{1,0:T(8,128)(2,1)} async-done(((bf16[32,1024]{1,0:T(8,128)(2,1)}), bf16[1024,1024]{1,0:T(8,128)(2,1)}) %all-gather.2.cloned.1.call-update) | async-done | bytes 2097168 | tf_op jit(solution)/shard_map/all_gather | solution.py:62
  94.8 2.4 fusion.55
  99.4 2.1 multiply_reduce_fusion.5
  102.1 2.1 multiply_reduce_fusion.4
  107.4 2.1 multiply_reduce_fusion.2
  117.2 109.3 %pmax.7 = bf16[1024,8]{0,1:T(8,128)(2,1)S(1)} all-reduce(bf16[1024,8]{0,1:T(8,128)(2,1)S(1)} %convert_element_type.107), channel_id=1, replica_groups=mesh['frame'=16,'tok'=32] {'tok'}, use_global_device_ids=true, to_apply=%region_8.0 | all-reduce | flops 8192 | bytes 32768 | tf_op jit(solution)/shard_map/pmax | solution.py:69
  226.5 3.6 fusion.58
  230.1 2.6 fusion.61
  232.7 2.6 fusion.64
  235.3 2.6 fusion.67
  237.8 2.6 fusion.70
  240.4 2.4 fusion.73
  242.9 2.4 fusion.76
  245.4 4.1 fusion.6
  249.5 112.8 %psum.15 = bf16[1024,8]{0,1:T(8,128)(2,1)S(1)} all-reduce(bf16[1024,8]{0,1:T(8,128)(2,1)S(1)} %get-tuple-element.5), channel_id=1, replica_groups=mesh['frame'=16,'tok'=32] {'tok'}, use_global_device_ids=true, to_apply=%region_18.0 | all-reduce | flops 8192 | bytes 32768 | tf_op jit(solution)/shard_map/psum | solution.py:78
  362.3 78.0 %all-reduce.2.cloned.1.call-done = bf16[1024,1024]{0,1:T(8,128)(2,1)} async-done(((bf16[1024,1024]{0,1:T(8,128)(2,1)}), bf16[1024,1024]{0,1:T(8,128)(2,1)}) %all-reduce.2.cloned.1.call-update) | async-done | bytes 2097168 | tf_op jit(solution)/shard_map/psum | solution.py:77
  440.3 2.2 fusion.5
  442.6 7.5 %collective-permute-start = (bf16[1024,1024]{0,1:T(8,128)(2,1)S(1)}, bf16[1024,1024]{0,1:T(8,128)(2,1)S(1)}, u32[]{:S(2)}, u32[]{:S(2)}) collective-permute-start(bf16[1024,1024]{0,1:T(8,128)(2,1)S(1)} %fusion.5), channel_id=1, source_target_pairs={{0,32},{32,64},{64,96},{96,128},{128,160},{160,192},{192,224},{224... | collective-permute-start | bytes 6291464 | tf_op jit(solution)/shard_map/ppermute | solution.py:14
  450.0 2.4 collective-permute-start.1
  452.5 40.5 %collective-permute-done = bf16[1024,1024]{0,1:T(8,128)(2,1)S(1)} collective-permute-done((bf16[1024,1024]{0,1:T(8,128)(2,1)S(1)}, bf16[1024,1024]{0,1:T(8,128)(2,1)S(1)}, u32[]{:S(2)}, u32[]{:S(2)}) %collective-permute-start) | collective-permute-done | bytes 2097184 | tf_op jit(solution)/shard_map/ppermute | solution.py:14
  492.9 27.8 %collective-permute-done.1 = bf16[1024,1024]{0,1:T(8,128)(2,1)S(1)} collective-permute-done((bf16[1024,1024]{0,1:T(8,128)(2,1)S(1)}, bf16[1024,1024]{0,1:T(8,128)(2,1)S(1)}, u32[]{:S(2)}, u32[]{:S(2)}) %collective-permute-start.1) | collective-permute-done | bytes 2097184 | tf_op jit(solution)/shard_map/ppermute | solution.py:14
  520.7 11.4 %fusion.1 = f32[1024]{0:T(1024)S(1)} fusion(bf16[1024,1024]{0,1:T(8,128)(2,1)S(1)} %collective-permute-done.1, bf16[1024,1024]{0,1:T(8,128)(2,1)S(1)} %collective-permute-done, bf16[1024,1024]{0,1:T(8,128)(2,1)S(1)} %fusion.5), kind=kLoop, calls=%fused_computation.3 | loop fusion | flops 25164800 | bytes 6295552 | tf_op jit(solution)/shard_map/reduce_sum | solution.py:85
  534.2 38.8 %all_to_all.5 = bf16[32,32,1024]{2,1,0:T(8,128)(2,1)S(1)} all-to-all(bf16[32,32,1024]{2,1,0:T(8,128)(2,1)S(1)} %stack.32), channel_id=1, replica_groups=mesh['frame'=16,'tok'=32] {'tok'}, dimensions={0} | all-to-all | bytes 4194304 | tf_op jit(solution)/shard_map/all_to_all | solution.py:90
  (85 shorter events, 27.4 us)
Async XLA Ops:
  6.5 1.6 copy-start
  6.5 86.0 %all-gather.2.cloned.1.call-start = ((), (), s32[]{:S(2)}) async-start(), calls=%async_computation.1 | async-start | bytes 2162688 | tf_op jit(solution)/shard_map/all_gather | solution.py:62
  7.3 433.1 %all-reduce.2.cloned.1.call-start = ((), (), s32[]{:S(2)}) async-start(), calls=%async_computation.2 | async-start | bytes 4194304 | tf_op jit(solution)/shard_map/psum | solution.py:77
  98.8 2.7 copy-start.1
  101.5 2.7 copy-start.2
  104.2 2.7 copy-start.4
  106.9 2.7 copy-start.6
  109.5 2.7 copy-start.8
  112.2 2.7 copy-start.10
  114.9 1.7 copy-start.12
  226.5 3.6 copy-start.3
  226.5 6.2 %copy-start.5 = (f32[768,1024]{1,0:T(8,128)S(1)}, f32[768,1024]{1,0:T(8,128)}, u32[]{:S(2)}) copy-start(f32[768,1024]{1,0:T(8,128)} %copy-done.4) | copy-start | bytes 9437188
  230.1 5.2 copy-start.7
  232.7 5.2 copy-start.9
  235.3 5.2 copy-start.11
  237.8 5.0 copy-start.13
  442.5 89.6 %copy-start.15 = (bf16[3072,32]{0,1:T(8,128)(2,1)S(1)}, bf16[3072,32]{0,1:T(8,128)(2,1)}, u32[]{:S(2)}) copy-start(bf16[3072,32]{0,1:T(8,128)(2,1)} %param.10) | copy-start | bytes 589828
  442.5 89.6 %copy-start.16 = (f32[3072]{0:T(1024)S(1)}, f32[3072]{0:T(1024)}, u32[]{:S(2)}) copy-start(f32[3072]{0:T(1024)} %param.9) | copy-start | bytes 36868
  442.6 50.4 %collective-permute-start = (bf16[1024,1024]{0,1:T(8,128)(2,1)S(1)}, bf16[1024,1024]{0,1:T(8,128)(2,1)S(1)}, u32[]{:S(2)}, u32[]{:S(2)}) collective-permute-start(bf16[1024,1024]{0,1:T(8,128)(2,1)S(1)} %fusion.5), channel_id=1, source_target_pairs={{0,32},{32,64},{64,96},{96,128},{128,160},{160,192},{192,224},{224... | collective-permute-start | bytes 6291464 | tf_op jit(solution)/shard_map/ppermute | solution.py:14
  450.0 70.7 %collective-permute-start.1 = (bf16[1024,1024]{0,1:T(8,128)(2,1)S(1)}, bf16[1024,1024]{0,1:T(8,128)(2,1)S(1)}, u32[]{:S(2)}, u32[]{:S(2)}) collective-permute-start(bf16[1024,1024]{0,1:T(8,128)(2,1)S(1)} %fusion.5), channel_id=1, source_target_pairs={{0,64},{32,96},{64,128},{96,160},{128,192},{160,224},{192,256},{22... | collective-permute-start | bytes 6291464 | tf_op jit(solution)/shard_map/ppermute | solution.py:14
  573.0 1.0 copy-start.14
Sparse Core Ops, SparseCore 0:
  10.5 82.0 all-gather.1
  249.6 190.6 all-reduce.1
